TPU v7x, 32 devices: a whole 2x2x4 slice. The times are simulated.
32 devices in a mesh: energy: 8 (over z, core), block: 4 (over y, x).
Axes of the slice: x: 2, y: 2, z: 4, core: 2. Of those that a mesh axis runs over, the one named last changes fastest.
Arguments:
- g_lesser: float32 [2, 8, 1024, 256], P(None, 'energy', 'block'), may hold values from -0.75 to 0.75
- g_greater: float32 [2, 8, 1024, 256], P(None, 'energy', 'block'), may hold values from -0.75 to 0.75
- onsite: float32 [2, 8, 1024, 256], P(None, 'energy', 'block'), may hold values from -1 to 7
- lower: float32 [2, 1024, 256], P(None, 'block'), may hold values from -0.5 to 2.7
- upper: float32 [2, 1024, 256], P(None, 'block'), may hold values from -0.5 to 2.7
- rhs: float32 [2, 8, 1024, 128], P(None, 'energy', 'block'), may hold values from -16 to 16
Outputs:
- solution: float32 [2, 8, 1024, 128], P(None, 'energy', 'block')
All inputs are finite; a program needn't handle non-finite values.
Results may differ from a plain program's by a relative error of at most 0.0003.
Values sent between devices are 32-bit elements; how exact they have to be, the bound alone decides.
A program may use at most 64 MiB of HBM per device.

v0:
```python
import math

import jax
import jax.numpy as jnp
from jax import lax
from jax.sharding import PartitionSpec as P

diagonal_guess = 5.0
MODE = lax.Precision.HIGH


def real_product(a, b):
    return jnp.matmul(a, b, precision=MODE)


def product(a, b):
    ar, ai = a
    br, bi = b
    return (
        real_product(ar, br) - real_product(ai, bi),
        real_product(ar, bi) + real_product(ai, br),
    )


def parts(a):
    return a[0], a[1]


def plus(a, b):
    return a[0] + b[0], a[1] + b[1]


def minus(a, b):
    return a[0] - b[0], a[1] - b[1]


def wide(*pieces):
    return tuple(jnp.concatenate([p[k] for p in pieces], axis=-1) for k in (0, 1))


def cut(a, start, stop):
    return a[0][:, start:stop], a[1][:, start:stop]


def remainder(matrix):
    eye = jnp.eye(matrix[0].shape[-1], dtype=jnp.float32)
    return eye - matrix[0] * (1.0 / diagonal_guess), -matrix[1] * (1.0 / diagonal_guess)


def inverse(matrix):
    eye = jnp.eye(matrix[0].shape[-1], dtype=jnp.float32)
    b = remainder(matrix)
    square = product(b, b)
    cube = product(b, square)
    scale = 1.0 / diagonal_guess
    return (eye + b[0] + square[0] + cube[0]) * scale, (b[1] + square[1] + cube[1]) * scale


def solve(matrix, source):
    b = remainder(matrix)
    value = source
    for _ in range(3):
        value = plus(source, product(b, value))
    scale = 1.0 / diagonal_guess
    return value[0] * scale, value[1] * scale


def convolve(lesser, greater):
    energies = lesser.shape[1]
    scale = 1.0 / math.sqrt(energies)
    out = []
    for w in range(energies):
        count = energies - w
        a, b = lesser[:, w:], greater[:, :count]
        out.append(
            jnp.stack(
                [
                    jnp.sum(a[0] * b[0] - a[1] * b[1], axis=0),
                    jnp.sum(a[0] * b[1] + a[1] * b[0], axis=0),
                ]
            )
            * scale
        )
    return jnp.stack(out, axis=1)


def shifted(value, steps):
    count = lax.axis_size("block")
    leading, last = max(0, -steps), min(count, count - steps)
    pairs = [(k, k + steps) for k in range(leading, last)]
    return lax.ppermute(value, "block", pairs)


def shards(g_lesser, g_greater, onsite, lower, upper, rhs):
    index = lax.axis_index("block")
    count = lax.axis_size("block")
    levels = count.bit_length() - 1
    n = onsite.shape[-1]
    both = jnp.concatenate(
        [jnp.where(index > 0, lower, 0.0), jnp.where(index < count - 1, upper, 0.0)], axis=-1
    )
    early_left, early_right = shifted(both, 1), shifted(both, -1)
    rhs_left, rhs_right = shifted(rhs, 1), shifted(rhs, -1)

    lesser = lax.all_to_all(g_lesser, "energy", split_axis=2, concat_axis=1, tiled=True)
    greater = lax.all_to_all(g_greater, "energy", split_axis=2, concat_axis=1, tiled=True)
    polar = lax.all_to_all(
        convolve(lesser, greater), "energy", split_axis=1, concat_axis=2, tiled=True
    )
    diag = parts((onsite - polar)[:, 0])
    low, up = cut(parts(both), 0, n), cut(parts(both), n, 2 * n)
    source = parts(rhs[:, 0])
    for depth in range(levels):
        stride = 1 << depth
        inv = inverse(diag)
        if depth == levels - 1:
            coupling = tuple(jnp.where(index < stride, up[k], low[k]) for k in (0, 1))
            sent = product(inv, wide(coupling, source))
            swap = [(k, k ^ stride) for k in range(count)]
            got = parts(lax.ppermute(jnp.stack(sent), "block", swap))
            change = product(coupling, got)
            diag = minus(diag, cut(change, 0, n))
            source = minus(source, cut(change, n, None))
        elif depth == 0:
            packed = jnp.stack(inv)
            inv_left, inv_right = parts(shifted(packed, 1)), parts(shifted(packed, -1))
            before, after = parts(early_left), parts(early_right)
            t = product(low, inv_left)
            change = product(t, wide(before, parts(rhs_left[:, 0])))
            w = product(up, inv_right)
            other = product(w, wide(after, parts(rhs_right[:, 0])))
            diag = minus(minus(diag, cut(change, n, 2 * n)), cut(other, 0, n))
            source = minus(minus(source, cut(change, 2 * n, None)), cut(other, 2 * n, None))
            low = tuple(-v for v in cut(change, 0, n))
            up = tuple(-v for v in cut(other, n, 2 * n))
        else:
            sent = jnp.stack(product(inv, wide(low, up, source)))
            left, right = parts(shifted(sent, stride)), parts(shifted(sent, -stride))
            change, other = product(low, left), product(up, right)
            diag = minus(minus(diag, cut(change, n, 2 * n)), cut(other, 0, n))
            source = minus(minus(source, cut(change, 2 * n, None)), cut(other, 2 * n, None))
            low = tuple(-v for v in cut(change, 0, n))
            up = tuple(-v for v in cut(other, n, 2 * n))
    return jnp.stack(solve(diag, source))[:, None]


def solution(mesh):
    placed = (
        P(None, "energy", "block", None),
        P(None, "energy", "block", None),
        P(None, "energy", "block", None),
        P(None, "block", None),
        P(None, "block", None),
        P(None, "energy", "block", None),
    )
    return jax.shard_map(
        shards,
        mesh=mesh,
        in_specs=placed,
        out_specs=P(None, "energy", "block", None),
        check_vma=False,
    )
```

profile of v0, /device:TPU:24, one launch (start us, length us, event | category | flops | bytes accessed | tf_op | source)
XLA Modules:
  0.0 153.8 jit_solution(13916684466820692516)
XLA Ops:
  0.0 2.3 %copy.27 = f32[2,1,256,256]{3,0,1,2:T(2,128)} copy(f32[2,1,256,256]{3,2,1,0:T(8,128)} %param.6) | data formatting | bytes 1048576 | tf_op args[0]
  2.3 5.2 %all-to-all-start = ((f32[2,1,256,256]{3,0,1,2:T(2,128)}), f32[2,1,256,256]{3,0,1,2:T(2,128)S(1)}, u32[]{:S(2)}, u32[]{:S(2)}) async-start(f32[2,1,256,256]{3,0,1,2:T(2,128)} %copy.27), calls=%async_computation | async-start | bytes 1048576 | tf_op jit(solution)/shard_map/all_to_all | solution.py:105
  7.5 1.2 copy.29
  8.7 11.6 %all-to-all-done = f32[2,1,256,256]{3,0,1,2:T(2,128)S(1)} async-done(((f32[2,1,256,256]{3,0,1,2:T(2,128)}), f32[2,1,256,256]{3,0,1,2:T(2,128)S(1)}, u32[]{:S(2)}, u32[]{:S(2)}) %all-to-all-start) | async-done | bytes 524320 | tf_op jit(solution)/shard_map/all_to_all | solution.py:105
  20.3 6.0 %all-to-all-start.1 = ((f32[2,1,256,256]{3,0,1,2:T(2,128)}), f32[2,1,256,256]{3,0,1,2:T(2,128)S(1)}, u32[]{:S(2)}, u32[]{:S(2)}) async-start(f32[2,1,256,256]{3,0,1,2:T(2,128)} %copy.29), calls=%async_computation.1 | async-start | bytes 1048576 | tf_op jit(solution)/shard_map/all_to_all | solution.py:106
  26.2 3.4 %collective-permute-start.2 = (f32[2,1,256,128]{3,2,1,0:T(8,128)}, f32[2,1,256,128]{3,2,1,0:T(8,128)S(1)}, u32[]{:S(2)}, u32[]{:S(2)}) collective-permute-start(f32[2,1,256,128]{3,2,1,0:T(8,128)} %param.11), channel_id=1, source_target_pairs={{0,1},{1,2},{2,3},{4,5},{5,6},{6,7},{8,9},{9,10},{10,11},{12,13},{... | collective-permute-start | bytes 786440 | tf_op jit(solution)/shard_map/ppermute | solution.py:91
  29.7 1.3 collective-permute-start.5
  31.0 8.0 %all-to-all-done.1 = f32[2,1,256,256]{3,0,1,2:T(2,128)S(1)} async-done(((f32[2,1,256,256]{3,0,1,2:T(2,128)}), f32[2,1,256,256]{3,0,1,2:T(2,128)S(1)}, u32[]{:S(2)}, u32[]{:S(2)}) %all-to-all-start.1) | async-done | bytes 524320 | tf_op jit(solution)/shard_map/all_to_all | solution.py:106
  39.4 0.4 fusion.121
  39.8 0.4 fusion.122
  40.5 0.8 copy.35
  41.3 6.1 %all-to-all-start.2 = ((f32[2,8,32,256]{3,2,0,1:T(8,128)}), f32[2,8,32,256]{3,2,0,1:T(8,128)S(1)}, u32[]{:S(2)}, u32[]{:S(2)}) async-start(f32[2,8,32,256]{3,2,0,1:T(8,128)} %copy.35), calls=%async_computation.2 | async-start | bytes 1048576 | tf_op jit(solution)/shard_map/all_to_all | solution.py:107
  47.7 4.4 %collective-permute-start.1 = (f32[2,256,512]{2,1,0:T(8,128)S(1)}, f32[2,256,512]{2,1,0:T(8,128)}, u32[]{:S(2)}, u32[]{:S(2)}) collective-permute-start(f32[2,256,512]{2,1,0:T(8,128)S(1)} %pad_maximum_fusion), channel_id=1, source_target_pairs={{0,1},{1,2},{2,3},{4,5},{5,6},{6,7},{8,9},{9,10},{10,11},{12,13},{... | collective-permute-start | bytes 3145736 | tf_op jit(solution)/shard_map/ppermute | solution.py:91
  52.1 1.3 collective-permute-start.4
  53.6 6.6 %all-to-all-done.2 = f32[2,8,32,256]{3,2,0,1:T(8,128)S(1)} async-done(((f32[2,8,32,256]{3,2,0,1:T(8,128)}), f32[2,8,32,256]{3,2,0,1:T(8,128)S(1)}, u32[]{:S(2)}, u32[]{:S(2)}) %all-to-all-start.2) | async-done | bytes 524320 | tf_op jit(solution)/shard_map/all_to_all | solution.py:107
  60.3 1.0 copy-done
  61.6 0.3 convolution_add_fusion.9
  62.2 0.3 fusion.48
  62.8 0.3 fusion.9
  63.8 3.4 %collective-permute-start = (f32[2,256,256]{2,1,0:T(8,128)S(1)}, f32[2,256,256]{2,1,0:T(8,128)S(1)}, u32[]{:S(2)}, u32[]{:S(2)}) collective-permute-start(f32[2,256,256]{2,1,0:T(8,128)S(1)} %pad_maximum_fusion.14), channel_id=1, source_target_pairs={{0,1},{1,2},{2,3},{4,5},{5,6},{6,7},{8,9},{9,10},{10,11},{12,13},{... | collective-permute-start | bytes 1572872 | tf_op jit(solution)/shard_map/ppermute | solution.py:91
  67.2 7.4 %collective-permute-done.1 = f32[2,256,512]{2,1,0:T(8,128)} collective-permute-done((f32[2,256,512]{2,1,0:T(8,128)S(1)}, f32[2,256,512]{2,1,0:T(8,128)}, u32[]{:S(2)}, u32[]{:S(2)}) %collective-permute-start.1) | collective-permute-done | bytes 1048608 | tf_op jit(solution)/shard_map/ppermute | solution.py:91
  74.6 1.3 slice_bitcast_fusion.2
  75.9 23.3 %collective-permute-done.4 = f32[2,256,512]{2,1,0:T(8,128)} collective-permute-done((f32[2,256,512]{2,1,0:T(8,128)S(1)}, f32[2,256,512]{2,1,0:T(8,128)}, u32[]{:S(2)}, u32[]{:S(2)}) %collective-permute-start.4) | collective-permute-done | bytes 1048608 | tf_op jit(solution)/shard_map/ppermute | solution.py:91
  99.2 1.3 slice_bitcast_fusion
  100.4 1.5 collective-permute-start.3
  102.5 0.5 fusion.24
  103.0 0.5 fusion.25
  104.1 0.5 convolution_subtract_fusion.1
  104.6 0.5 convolution_add_fusion.1
  105.1 15.5 %collective-permute-done.3 = f32[2,256,256]{2,1,0:T(8,128)S(1)} collective-permute-done((f32[2,256,256]{2,1,0:T(8,128)S(1)}, f32[2,256,256]{2,1,0:T(8,128)S(1)}, u32[]{:S(2)}, u32[]{:S(2)}) %collective-permute-start.3) | collective-permute-done | bytes 524320 | tf_op jit(solution)/shard_map/ppermute | solution.py:91
  121.2 0.5 fusion.22
  121.8 0.5 fusion.23
  122.9 0.5 convolution_subtract_fusion
  123.4 0.5 convolution_add_fusion
  123.9 1.0 slice_subtract_fusion.10
  125.1 0.3 fusion.92
  125.7 0.3 convolution_add_fusion.5
  127.2 0.3 fusion.10
  127.5 0.4 fusion.32
  127.9 0.4 fusion.33
  128.3 0.4 fusion
  128.7 0.4 fusion.1
  129.2 18.7 %collective-permute-done.6 = f32[2,256,384]{2,1,0:T(8,128)S(1)} collective-permute-done((f32[2,256,384]{2,1,0:T(8,128)S(1)}, f32[2,256,384]{2,1,0:T(8,128)S(1)}, u32[]{:S(2)}, u32[]{:S(2)}) %collective-permute-start.6) | collective-permute-done | bytes 786464 | tf_op jit(solution)/shard_map/ppermute | solution.py:120
  147.9 0.4 fusion.30
  148.3 0.4 convolution_add_fusion.2
  148.8 0.4 fusion.31
  149.1 0.4 convolution_subtract_fusion.2
  153.0 0.7 maximum_bitcast_fusion
  (75 shorter events, 9.9 us)
Async XLA Ops:
  2.3 5.2 %copy-start.1 = (f32[2,1,256,256]{3,2,1,0:T(8,128)S(1)}, f32[2,1,256,256]{3,2,1,0:T(8,128)}, u32[]{:S(2)}) copy-start(f32[2,1,256,256]{3,2,1,0:T(8,128)} %param.7) | copy-start | bytes 1572868
  2.3 18.0 %all-to-all-start = ((f32[2,1,256,256]{3,0,1,2:T(2,128)}), f32[2,1,256,256]{3,0,1,2:T(2,128)S(1)}, u32[]{:S(2)}, u32[]{:S(2)}) async-start(f32[2,1,256,256]{3,0,1,2:T(2,128)} %copy.27), calls=%async_computation | async-start | bytes 1048576 | tf_op jit(solution)/shard_map/all_to_all | solution.py:105
  20.3 18.7 %all-to-all-start.1 = ((f32[2,1,256,256]{3,0,1,2:T(2,128)}), f32[2,1,256,256]{3,0,1,2:T(2,128)S(1)}, u32[]{:S(2)}, u32[]{:S(2)}) async-start(f32[2,1,256,256]{3,0,1,2:T(2,128)} %copy.29), calls=%async_computation.1 | async-start | bytes 1048576 | tf_op jit(solution)/shard_map/all_to_all | solution.py:106
  26.2 27.3 %collective-permute-start.2 = (f32[2,1,256,128]{3,2,1,0:T(8,128)}, f32[2,1,256,128]{3,2,1,0:T(8,128)S(1)}, u32[]{:S(2)}, u32[]{:S(2)}) collective-permute-start(f32[2,1,256,128]{3,2,1,0:T(8,128)} %param.11), channel_id=1, source_target_pairs={{0,1},{1,2},{2,3},{4,5},{5,6},{6,7},{8,9},{9,10},{10,11},{12,13},{... | collective-permute-start | bytes 786440 | tf_op jit(solution)/shard_map/ppermute | solution.py:91
  29.7 24.0 %collective-permute-start.5 = (f32[2,1,256,128]{3,2,1,0:T(8,128)}, f32[2,1,256,128]{3,2,1,0:T(8,128)S(1)}, u32[]{:S(2)}, u32[]{:S(2)}) collective-permute-start(f32[2,1,256,128]{3,2,1,0:T(8,128)} %param.11), channel_id=1, source_target_pairs={{1,0},{2,1},{3,2},{5,4},{6,5},{7,6},{9,8},{10,9},{11,10},{13,12},{... | collective-permute-start | bytes 786440 | tf_op jit(solution)/shard_map/ppermute | solution.py:91
  41.3 6.1 %copy-start.2 = (f32[2,256,256]{2,1,0:T(8,128)S(1)}, f32[2,256,256]{2,1,0:T(8,128)}, u32[]{:S(2)}) copy-start(f32[2,256,256]{2,1,0:T(8,128)} %param.10) | copy-start | bytes 1572868
  41.3 6.1 %copy-start.3 = (f32[2,256,256]{2,1,0:T(8,128)S(1)}, f32[2,256,256]{2,1,0:T(8,128)}, u32[]{:S(2)}) copy-start(f32[2,256,256]{2,1,0:T(8,128)} %param.9) | copy-start | bytes 1572868
  41.3 18.9 %all-to-all-start.2 = ((f32[2,8,32,256]{3,2,0,1:T(8,128)}), f32[2,8,32,256]{3,2,0,1:T(8,128)S(1)}, u32[]{:S(2)}, u32[]{:S(2)}) async-start(f32[2,8,32,256]{3,2,0,1:T(8,128)} %copy.35), calls=%async_computation.2 | async-start | bytes 1048576 | tf_op jit(solution)/shard_map/all_to_all | solution.py:107
  47.7 26.9 %collective-permute-start.1 = (f32[2,256,512]{2,1,0:T(8,128)S(1)}, f32[2,256,512]{2,1,0:T(8,128)}, u32[]{:S(2)}, u32[]{:S(2)}) collective-permute-start(f32[2,256,512]{2,1,0:T(8,128)S(1)} %pad_maximum_fusion), channel_id=1, source_target_pairs={{0,1},{1,2},{2,3},{4,5},{5,6},{6,7},{8,9},{9,10},{10,11},{12,13},{... | collective-permute-start | bytes 3145736 | tf_op jit(solution)/shard_map/ppermute | solution.py:91
  52.1 47.0 %collective-permute-start.4 = (f32[2,256,512]{2,1,0:T(8,128)S(1)}, f32[2,256,512]{2,1,0:T(8,128)}, u32[]{:S(2)}, u32[]{:S(2)}) collective-permute-start(f32[2,256,512]{2,1,0:T(8,128)S(1)} %pad_maximum_fusion), channel_id=1, source_target_pairs={{1,0},{2,1},{3,2},{5,4},{6,5},{7,6},{9,8},{10,9},{11,10},{13,12},{... | collective-permute-start | bytes 3145736 | tf_op jit(solution)/shard_map/ppermute | solution.py:91
  60.2 1.0 copy-start
  63.8 38.1 %collective-permute-start = (f32[2,256,256]{2,1,0:T(8,128)S(1)}, f32[2,256,256]{2,1,0:T(8,128)S(1)}, u32[]{:S(2)}, u32[]{:S(2)}) collective-permute-start(f32[2,256,256]{2,1,0:T(8,128)S(1)} %pad_maximum_fusion.14), channel_id=1, source_target_pairs={{0,1},{1,2},{2,3},{4,5},{5,6},{6,7},{8,9},{9,10},{10,11},{12,13},{... | collective-permute-start | bytes 1572872 | tf_op jit(solution)/shard_map/ppermute | solution.py:91
  100.4 20.2 %collective-permute-start.3 = (f32[2,256,256]{2,1,0:T(8,128)S(1)}, f32[2,256,256]{2,1,0:T(8,128)S(1)}, u32[]{:S(2)}, u32[]{:S(2)}) collective-permute-start(f32[2,256,256]{2,1,0:T(8,128)S(1)} %pad_maximum_fusion.14), channel_id=1, source_target_pairs={{1,0},{2,1},{3,2},{5,4},{6,5},{7,6},{9,8},{10,9},{11,10},{13,12},{... | collective-permute-start | bytes 1572872 | tf_op jit(solution)/shard_map/ppermute | solution.py:91
  129.1 18.8 %collective-permute-start.6 = (f32[2,256,384]{2,1,0:T(8,128)S(1)}, f32[2,256,384]{2,1,0:T(8,128)S(1)}, u32[]{:S(2)}, u32[]{:S(2)}) collective-permute-start(f32[2,256,384]{2,1,0:T(8,128)S(1)} %pad_maximum_fusion.1), channel_id=1, source_target_pairs={{0,2},{1,3},{2,0},{3,1},{4,6},{5,7},{6,4},{7,5},{8,10},{9,11},{10,... | collective-permute-start | bytes 2359304 | tf_op jit(solution)/shard_map/ppermute | solution.py:120
where the time goes:
time: 156 us; the launch traced here: 154 us
  waiting for transfers between devices  91.1 us (58%)
  starting transfers between devices  32.7 us (21%)
  matrix products  17.5 us (11%)
  local copies, waits for them, and re-layouts  8.79 us (6%)
  other arithmetic  2.98 us (2%)
    ppermute x6, waiting for transfers between devices, shifted(): return lax.ppermute(value, 'block', pairs)  46.2 us
    ppermute x1, waiting for transfers between devices, shards(): got = parts(lax.ppermute(jnp.stack(sent), 'block', swap))  18.7 us
    dot_general x52, matrix products, real_product(): return jnp.matmul(a, b, precision=MODE)  17.5 us
    ppermute x6, starting transfers between devices, shifted(): return lax.ppermute(value, 'block', pairs)  15.3 us
    all_to_all x1, waiting for transfers between devices, shards(): lax.all_to_all(g_lesser, 'energy', split_axis=2, concat_axis=1, tiled=True)  11.6 us
    all_to_all x1, waiting for transfers between devices, shards(): lax.all_to_all(g_greater, 'energy', split_axis=2, concat_axis=1, tiled=True)  8 us
    all_to_all x1, waiting for transfers between devices, shards(): lax.all_to_all(convolve(lesser, greater), 'energy', split_axis=1, concat_...  6.57 us
    all_to_all x1, starting transfers between devices, shards(): lax.all_to_all(convolve(lesser, greater), 'energy', split_axis=1, concat_...  6.12 us
  transfers between devices with their start and end apart: 10, of which 7 were waited for; matrix products, arithmetic and copies ran while one was open for 8% of the time, Pallas kernels for 0%

commit v1 on v0

--- a/solution.py
+++ b/solution.py
@@ -3,10 +3,13 @@
 import jax
 import jax.numpy as jnp
 from jax import lax
+from jax.experimental import pallas as pl
+from jax.experimental.pallas import tpu as pltpu
 from jax.sharding import PartitionSpec as P
 
 diagonal_guess = 5.0
 MODE = lax.Precision.HIGH
+MESH = pl.DeviceIdType.MESH
 
 
 def real_product(a, b):
@@ -65,23 +68,195 @@
     return value[0] * scale, value[1] * scale
 
 
-def convolve(lesser, greater):
-    energies = lesser.shape[1]
+def front_kernel(
+    gl, gg, onsite, lower, upper, rhs, diag, near_lu, near_s,
+    lu, gl_all, gg_all, res, pol,
+    in_send, in_recv, out_send, out_recv, lu_send, lu_recv, hop_send, hop_recv,
+    mate_send, mate_recv, local,
+):
+    e, i = lax.axis_index("energy"), lax.axis_index("block")
+    energies, count = lax.axis_size("energy"), lax.axis_size("block")
+    share = gl.shape[2] // energies
+    c, p = lax.rem(e, 2), lax.rem(i, 2)
+    mate, side = e + 1 - 2 * c, 1 - p
+    pair, onward, behind = i + 1 - 2 * p, i + 2 - 4 * p, i - 2 + 4 * p
+    has_onward = jnp.logical_and(onward >= 0, onward < count)
+    has_behind = jnp.logical_and(behind >= 0, behind < count)
+
+    fill = [pltpu.make_async_copy((lower, upper)[k], lu.at[k], local.at[k]) for k in (0, 1)]
+    for copy in fill:
+        copy.start()
+    barrier = pltpu.get_barrier_semaphore()
+    for k in range(1, energies):
+        pl.semaphore_signal(barrier, inc=1, device_id={"energy": lax.rem(e + k, energies)}, device_id_type=MESH)
+    pl.semaphore_signal(barrier, inc=1, device_id={"block": pair}, device_id_type=MESH)
+
+    @pl.when(has_onward)
+    def _():
+        pl.semaphore_signal(barrier, inc=1, device_id={"block": onward}, device_id_type=MESH)
+
+    @pl.when(has_behind)
+    def _():
+        pl.semaphore_signal(barrier, inc=1, device_id={"block": behind}, device_id_type=MESH)
+
+    pl.semaphore_wait(barrier, energies + has_onward.astype(jnp.int32) + has_behind.astype(jnp.int32))
+
+    def remote(src, dst, send, recv, **where):
+        return pltpu.make_async_remote_copy(
+            src_ref=src, dst_ref=dst, send_sem=send, recv_sem=recv, device_id=where, device_id_type=MESH
+        )
+
+    def in_copy(k, q, source):
+        src, dst = ((gl, gl_all), (gg, gg_all))[k]
+        rows = src.at[:, 0, pl.ds(q * share, share), :]
+        return remote(rows, dst.at[source], in_send.at[k, q], in_recv.at[k, source], energy=q)
+
+    def out_copy(w, source):
+        return remote(res.at[w], pol.at[source], out_send.at[w], out_recv.at[source], energy=w)
+
+    for copy in fill:
+        copy.wait()
+    for k in (0, 1):
+        for q in range(energies):
+
+            @pl.when(q != e)
+            def _():
+                in_copy(k, q, e).start()
+
+    own = []
+    for k, (src, dst) in enumerate(((gl, gl_all), (gg, gg_all))):
+        rows = src.at[:, 0, pl.ds(pl.multiple_of(e * share, 8), share), :]
+        own.append(pltpu.make_async_copy(rows, dst.at[e], local.at[k]))
+        own[-1].start()
+
+    mine = (lu.at[c, 0], lu.at[c, 1], rhs.at[:, 0])
+
+    def slot(s, k):
+        return near_s.at[s] if k == 2 else near_lu.at[s, c, k]
+
+    direct = [remote(mine[k], slot(p, k), lu_send.at[k], lu_recv.at[k], block=pair) for k in range(3)]
+    hops = [remote(slot(side, k), slot(p, k), hop_send.at[k], hop_recv.at[k], block=onward) for k in range(3)]
+    for copy in direct:
+        copy.start()
+    shared = [
+        remote(slot(s, k), slot(s, k), mate_send.at[j, k], mate_recv.at[j, k], energy=mate)
+        for j, s in enumerate((side, p))
+        for k in (0, 1)
+    ]
+    for k in range(3):
+        direct[k].wait_recv()
+
+        @pl.when(has_onward)
+        def _():
+            hops[k].start()
+
+        if k < 2:
+            shared[k].start()
+
+    for copy in own:
+        copy.wait()
+    for k in (0, 1):
+        for q in range(energies):
+
+            @pl.when(q != e)
+            def _():
+                in_copy(k, q, q).wait_recv()
+
     scale = 1.0 / math.sqrt(energies)
-    out = []
-    for w in range(energies):
-        count = energies - w
-        a, b = lesser[:, w:], greater[:, :count]
-        out.append(
-            jnp.stack(
-                [
-                    jnp.sum(a[0] * b[0] - a[1] * b[1], axis=0),
-                    jnp.sum(a[0] * b[1] + a[1] * b[0], axis=0),
-                ]
-            )
-            * scale
-        )
-    return jnp.stack(out, axis=1)
+    for w in list(range(energies)):
+
+        def step(row, carry, w=w):
+            rows = pl.ds(pl.multiple_of(row * 8, 8), 8)
+            real = imag = None
+            for k in range(w, energies):
+                a, b = gl_all[k, 0, rows], gl_all[k, 1, rows]
+                x, y = gg_all[k - w, 0, rows], gg_all[k - w, 1, rows]
+                s, t = a * x - b * y, a * y + b * x
+                real, imag = (s, t) if real is None else (real + s, imag + t)
+            res[w, 0, rows] = real * scale
+            res[w, 1, rows] = imag * scale
+            return carry
+
+        lax.fori_loop(0, share // 8, step, 0)
+
+        @pl.when(w != e)
+        def _():
+            out_copy(w, e).start()
+
+    keep = pltpu.make_async_copy(res.at[e], pol.at[e], local.at[0])
+    keep.start()
+
+    @pl.when(has_behind)
+    def _():
+        for k in range(3):
+            hops[k].wait_recv()
+            if k < 2:
+                shared[2 + k].start()
+
+    keep.wait()
+    for q in range(energies):
+
+        @pl.when(q != e)
+        def _():
+            out_copy(q, q).wait_recv()
+
+        rows = pl.ds(q * share, share)
+        for k in (0, 1):
+            diag[k, rows] = onsite[k, 0, rows] - pol[q, k]
+
+    for k in range(2):
+        shared[k].wait_recv()
+
+    @pl.when(has_behind)
+    def _():
+        for k in range(2):
+            shared[2 + k].wait()
+
+    for k in range(2):
+        shared[k].wait_send()
+    for k in range(3):
+        direct[k].wait_send()
+
+        @pl.when(has_onward)
+        def _():
+            hops[k].wait_send()
+
+    for q in range(energies):
+
+        @pl.when(q != e)
+        def _():
+            in_copy(0, q, e).wait_send()
+            in_copy(1, q, e).wait_send()
+            out_copy(q, e).wait_send()
+
+
+def front(g_lesser, g_greater, onsite, lower, upper, rhs):
+    energies = lax.axis_size("energy")
+    n, columns = onsite.shape[2], rhs.shape[-1]
+    share = n // energies
+    vmem = pl.BlockSpec(memory_space=pltpu.VMEM)
+    f32 = jnp.float32
+    dma = pltpu.SemaphoreType.DMA
+    pieces = pltpu.VMEM((energies, 2, share, n), f32)
+    return pl.pallas_call(
+        front_kernel,
+        name="front",
+        out_shape=(
+            jax.ShapeDtypeStruct((2, n, n), f32),
+            jax.ShapeDtypeStruct((2, 2, 2, n, n), f32),
+            jax.ShapeDtypeStruct((2, 2, n, columns), f32),
+        ),
+        in_specs=[vmem] * 6,
+        out_specs=(vmem,) * 3,
+        scratch_shapes=[
+            pltpu.VMEM((2, 2, n, n), f32),
+            pieces, pieces, pieces, pieces,
+            dma((2, energies)), dma((2, energies)), dma((energies,)), dma((energies,)),
+            dma((3,)), dma((3,)), dma((3,)), dma((3,)),
+            dma((2, 2)), dma((2, 2)), dma((2,)),
+        ],
+        compiler_params=pltpu.CompilerParams(collective_id=0, has_side_effects=True),
+    )(g_lesser, g_greater, onsite, lower, upper, rhs)
 
 
 def shifted(value, steps):
@@ -99,15 +274,9 @@
     both = jnp.concatenate(
         [jnp.where(index > 0, lower, 0.0), jnp.where(index < count - 1, upper, 0.0)], axis=-1
     )
-    early_left, early_right = shifted(both, 1), shifted(both, -1)
-    rhs_left, rhs_right = shifted(rhs, 1), shifted(rhs, -1)
-
-    lesser = lax.all_to_all(g_lesser, "energy", split_axis=2, concat_axis=1, tiled=True)
-    greater = lax.all_to_all(g_greater, "energy", split_axis=2, concat_axis=1, tiled=True)
-    polar = lax.all_to_all(
-        convolve(lesser, greater), "energy", split_axis=1, concat_axis=2, tiled=True
-    )
-    diag = parts((onsite - polar)[:, 0])
+    diag, near_lu, near_s = front(g_lesser, g_greater, onsite, lower, upper, rhs)
+    diag = parts(diag)
+    first, final = index < 2, index >= count - 2
     low, up = cut(parts(both), 0, n), cut(parts(both), n, 2 * n)
     source = parts(rhs[:, 0])
     for depth in range(levels):
@@ -124,15 +293,16 @@
         elif depth == 0:
             packed = jnp.stack(inv)
             inv_left, inv_right = parts(shifted(packed, 1)), parts(shifted(packed, -1))
-            before, after = parts(early_left), parts(early_right)
-            t = product(low, inv_left)
-            change = product(t, wide(before, parts(rhs_left[:, 0])))
-            w = product(up, inv_right)
-            other = product(w, wide(after, parts(rhs_right[:, 0])))
+            t, w = product(low, inv_left), product(up, inv_right)
+            lu_l, lu_r = near_lu[0], near_lu[1]
+            change = product(t, wide(parts(lu_l[0]), parts(lu_l[1]), parts(near_s[0])))
+            other = product(w, wide(parts(lu_r[0]), parts(lu_r[1]), parts(near_s[1])))
+            change = tuple(jnp.where(index > 0, v, 0.0) for v in change)
+            other = tuple(jnp.where(index < count - 1, v, 0.0) for v in other)
             diag = minus(minus(diag, cut(change, n, 2 * n)), cut(other, 0, n))
             source = minus(minus(source, cut(change, 2 * n, None)), cut(other, 2 * n, None))
-            low = tuple(-v for v in cut(change, 0, n))
-            up = tuple(-v for v in cut(other, n, 2 * n))
+            low = tuple(jnp.where(first, 0.0, -v) for v in cut(change, 0, n))
+            up = tuple(jnp.where(final, 0.0, -v) for v in cut(other, n, 2 * n))
         else:
             sent = jnp.stack(product(inv, wide(low, up, source)))
             left, right = parts(shifted(sent, stride)), parts(shifted(sent, -stride))

time: 156 us -> 113 us (0.72)
  waiting for transfers between devices: 91.1 us -> 27.6 us
  Pallas kernels: 0 us -> 42.5 us
  starting transfers between devices: 32.7 us -> 17.6 us
  local copies, waits for them, and re-layouts: 8.79 us -> 1.69 us
  matrix products: 17.5 us -> 20.7 us
  other arithmetic: 2.98 us -> 1.35 us
    pallas_call x0 -> x1, Pallas kernels: none -> 42.5 us  [front(): pl.pallas_call(front_kernel, name='front', out_shape=(jax.ShapeDtypeStruc...]
    ppermute x6 -> x2, waiting for transfers between devices: 46.2 us -> 9.83 us  [shifted(): return lax.ppermute(value, 'block', pairs)]
    all_to_all x3 -> x0, waiting for transfers between devices: 26.2 us -> none  [the longest x1 11.6 us: shards(): lax.all_to_all(g_lesser, 'energy', split_axis=2, concat_axis=1, tiled=True)]
    all_to_all x3 -> x0, starting transfers between devices: 17.3 us -> none  [the longest x1 6.12 us: shards(): lax.all_to_all(convolve(lesser, greater), 'energy', split_axis=1, concat_...]
    ppermute x1, starting transfers between devices: 0.07 us -> 11.6 us  [shards(): got = parts(lax.ppermute(jnp.stack(sent), 'block', swap))]
    ppermute x6 -> x2, starting transfers between devices: 15.3 us -> 6.05 us  [shifted(): return lax.ppermute(value, 'block', pairs)]
    dot_general x52, matrix products: 17.5 us -> 20.7 us  [real_product(): return jnp.matmul(a, b, precision=MODE)]
    unnamed x10 -> x12, local copies, waits for them, and re-layouts: 4.46 us -> 1.52 us
  transfers between devices with their start and end apart: 10 -> 3, of which waited for: 7 -> 2; matrix products, arithmetic and copies ran while one was open for 8% -> 3% of each run, Pallas kernels for 0% -> 0%
where the time goes in v1:
time: 113 us; the launch traced here: 112 us
  Pallas kernels  42.5 us (38%)
  waiting for transfers between devices  27.6 us (24%)
  matrix products  20.7 us (18%)
  starting transfers between devices  17.6 us (16%)
  local copies, waits for them, and re-layouts  1.69 us (1%)
  other arithmetic  1.35 us (1%)
    pallas_call x1, Pallas kernels, front(): pl.pallas_call(front_kernel, name='front', out_shape=(jax.ShapeDtypeStruc...  42.5 us
    dot_general x52, matrix products, real_product(): return jnp.matmul(a, b, precision=MODE)  20.7 us
    ppermute x1, waiting for transfers between devices, shards(): got = parts(lax.ppermute(jnp.stack(sent), 'block', swap))  17.8 us
    ppermute x1, starting transfers between devices, shards(): got = parts(lax.ppermute(jnp.stack(sent), 'block', swap))  11.6 us
    ppermute x2, waiting for transfers between devices, shifted(): return lax.ppermute(value, 'block', pairs)  9.83 us
    ppermute x2, starting transfers between devices, shifted(): return lax.ppermute(value, 'block', pairs)  6.05 us
  transfers between devices with their start and end apart: 3, of which 2 were waited for; matrix products, arithmetic and copies ran while one was open for 3% of the time, Pallas kernels for 0%

profile of v1, /device:TPU:24, one launch (start us, length us, event | category | flops | bytes accessed | tf_op | source)
XLA Modules:
  0.0 112.1 jit_solution(16507362547536329557)
XLA Ops:
  0.0 42.5 %front.1 = (f32[2,256,256]{2,1,0:T(8,128)}, f32[2,2,2,256,256]{4,3,2,1,0:T(8,128)}, f32[2,2,256,128]{3,2,1,0:T(8,128)}) custom-call(f32[2,1,256,256]{3,2,1,0:T(8,128)} %gl.1, f32[2,1,256,256]{3,2,1,0:T(8,128)} %gg.1, f32[2,1,256,256]{3,2,1,0:T(8,128)} %onsite.1, f32[2,256,256]{2,1,0:T(8,128)} %lower.1, f32[2,256,256]{2,1,0:T(8,128)} %upper.1, ...), custom_call_target="tpu_custom_call" | custom-call | tf_op jit(solution)/shard_map/front/pallas_call | solution.py:241
  42.5 1.4 %fusion.50 = f32[256,256]{1,0:T(8,128)S(1)} fusion(f32[2,256,256]{2,1,0:T(8,128)} %get-tuple-element.8), kind=kOutput, calls=%fused_computation.110 | convolution fusion | flops 101056512 | bytes 786432 | tf_op jit(solution)/shard_map/dot_general | solution.py:16
  43.9 1.3 %fusion.55 = f32[256,256]{1,0:T(8,128)S(1)} fusion(f32[2,256,256]{2,1,0:T(8,128)} %get-tuple-element.8), kind=kOutput, calls=%fused_computation.115 | convolution fusion | flops 100925440 | bytes 524288 | tf_op jit(solution)/shard_map/dot_general | solution.py:16
  45.2 1.3 %convolution_add_fusion.9 = f32[256,256]{1,0:T(8,128)S(1)} fusion(f32[256,256]{1,0:T(8,128)S(1)} %fusion.50, f32[2,256,256]{2,1,0:T(8,128)} %get-tuple-element.8), kind=kOutput, calls=%fused_computation.28 | convolution fusion | flops 101122048 | bytes 1048576 | tf_op jit(solution)/shard_map/dot_general | solution.py:16
  46.6 0.3 fusion.74
  46.9 0.3 convolution_subtract_fusion.9
  47.2 0.3 fusion.75
  47.5 0.3 fusion.13
  47.8 0.3 fusion.11
  48.1 1.3 %collective-permute-start.1 = (f32[2,256,256]{2,1,0:T(8,128)S(1)}, f32[2,256,256]{2,1,0:T(8,128)S(1)}, u32[]{:S(2)}, u32[]{:S(2)}) collective-permute-start(f32[2,256,256]{2,1,0:T(8,128)S(1)} %pad_maximum_fusion.6), channel_id=1, source_target_pairs={{1,0},{2,1},{3,2},{5,4},{6,5},{7,6},{9,8},{10,9},{11,10},{13,12},{... | collective-permute-start | bytes 1572872 | tf_op jit(solution)/shard_map/ppermute | solution.py:266
  49.4 4.8 %collective-permute-start = (f32[2,256,256]{2,1,0:T(8,128)S(1)}, f32[2,256,256]{2,1,0:T(8,128)S(1)}, u32[]{:S(2)}, u32[]{:S(2)}) collective-permute-start(f32[2,256,256]{2,1,0:T(8,128)S(1)} %pad_maximum_fusion.6), channel_id=1, source_target_pairs={{0,1},{1,2},{2,3},{4,5},{5,6},{6,7},{8,9},{9,10},{10,11},{12,13},{... | collective-permute-start | bytes 1572872 | tf_op jit(solution)/shard_map/ppermute | solution.py:266
  54.5 0.8 copy-done.5
  55.3 0.7 copy-done.1
  56.1 9.8 %collective-permute-done = f32[2,256,256]{2,1,0:T(8,128)S(1)} collective-permute-done((f32[2,256,256]{2,1,0:T(8,128)S(1)}, f32[2,256,256]{2,1,0:T(8,128)S(1)}, u32[]{:S(2)}, u32[]{:S(2)}) %collective-permute-start) | collective-permute-done | bytes 524320 | tf_op jit(solution)/shard_map/ppermute | solution.py:266
  66.5 0.5 fusion.31
  67.1 0.5 fusion.32
  68.2 0.5 fusion.2
  68.7 0.5 fusion
  69.8 0.5 fusion.29
  70.4 0.5 fusion.30
  71.5 0.5 fusion.3
  72.0 0.5 fusion.1
  72.8 0.3 fusion.91
  73.1 0.3 fusion.73
  73.4 0.3 convolution_add_fusion.5
  73.7 0.3 fusion.89
  74.0 0.3 convolution_subtract_fusion.5
  74.3 0.3 fusion.90
  74.6 0.3 fusion.15
  74.9 0.3 fusion.14
  75.2 0.4 fusion.35
  75.6 0.4 fusion.36
  76.0 0.4 fusion.4
  76.4 0.4 fusion.5
  76.8 11.6 %collective-permute-start.2 = (f32[2,256,384]{2,1,0:T(8,128)S(1)}, f32[2,256,384]{2,1,0:T(8,128)S(1)}, u32[]{:S(2)}, u32[]{:S(2)}) collective-permute-start(f32[2,256,384]{2,1,0:T(8,128)S(1)} %pad_maximum_fusion), channel_id=1, source_target_pairs={{0,2},{1,3},{2,0},{3,1},{4,6},{5,7},{6,4},{7,5},{8,10},{9,11},{10,... | collective-permute-start | bytes 2359304 | tf_op jit(solution)/shard_map/ppermute | solution.py:289
  88.4 17.8 %collective-permute-done.2 = f32[2,256,384]{2,1,0:T(8,128)S(1)} collective-permute-done((f32[2,256,384]{2,1,0:T(8,128)S(1)}, f32[2,256,384]{2,1,0:T(8,128)S(1)}, u32[]{:S(2)}, u32[]{:S(2)}) %collective-permute-start.2) | collective-permute-done | bytes 786464 | tf_op jit(solution)/shard_map/ppermute | solution.py:289
  106.2 0.4 fusion.33
  106.6 0.4 convolution_add_fusion.2
  107.1 0.4 fusion.34
  107.5 0.4 convolution_subtract_fusion.2
  107.9 0.3 fusion.120
  108.2 0.3 fusion.122
  108.5 0.3 fusion.25
  109.7 0.3 fusion.23
  109.9 0.3 fusion.22
  110.8 0.3 fusion.18
  111.1 0.3 fusion.21
  111.4 0.7 maximum_bitcast_fusion
  (36 shorter events, 4.4 us)
Async XLA Ops:
  42.5 4.0 %copy-start = (f32[2,256,256]{2,1,0:T(8,128)S(1)}, f32[2,256,256]{2,1,0:T(8,128)}, u32[]{:S(2)}) copy-start(f32[2,256,256]{2,1,0:T(8,128)} %get-tuple-element.8) | copy-start | bytes 1572868
  47.1 7.0 %copy-start.2 = (f32[2,256,256]{2,1,0:T(8,128)S(1)}, f32[2,256,256]{2,1,0:T(8,128)}, u32[]{:S(2)}) copy-start(f32[2,256,256]{2,1,0:T(8,128)} %lower.1) | copy-start | bytes 1572868
  47.2 7.0 %copy-start.3 = (f32[2,256,256]{2,1,0:T(8,128)S(1)}, f32[2,256,256]{2,1,0:T(8,128)}, u32[]{:S(2)}) copy-start(f32[2,256,256]{2,1,0:T(8,128)} %upper.1) | copy-start | bytes 1572868
  48.1 21.1 %collective-permute-start.1 = (f32[2,256,256]{2,1,0:T(8,128)S(1)}, f32[2,256,256]{2,1,0:T(8,128)S(1)}, u32[]{:S(2)}, u32[]{:S(2)}) collective-permute-start(f32[2,256,256]{2,1,0:T(8,128)S(1)} %pad_maximum_fusion.6), channel_id=1, source_target_pairs={{1,0},{2,1},{3,2},{5,4},{6,5},{7,6},{9,8},{10,9},{11,10},{13,12},{... | collective-permute-start | bytes 1572872 | tf_op jit(solution)/shard_map/ppermute | solution.py:266
  49.4 16.6 %collective-permute-start = (f32[2,256,256]{2,1,0:T(8,128)S(1)}, f32[2,256,256]{2,1,0:T(8,128)S(1)}, u32[]{:S(2)}, u32[]{:S(2)}) collective-permute-start(f32[2,256,256]{2,1,0:T(8,128)S(1)} %pad_maximum_fusion.6), channel_id=1, source_target_pairs={{0,1},{1,2},{2,3},{4,5},{5,6},{6,7},{8,9},{9,10},{10,11},{12,13},{... | collective-permute-start | bytes 1572872 | tf_op jit(solution)/shard_map/ppermute | solution.py:266
  54.2 1.0 copy-start.5
  54.3 1.7 %copy-start.1 = (f32[2,2,2,256,256]{4,3,2,1,0:T(8,128)S(1)}, f32[2,2,2,256,256]{4,3,2,1,0:T(8,128)}, u32[]{:S(2)}) copy-start(f32[2,2,2,256,256]{4,3,2,1,0:T(8,128)} %get-tuple-element.9) | copy-start | bytes 6291460
  71.5 1.1 copy-start.4
  76.8 29.4 %collective-permute-start.2 = (f32[2,256,384]{2,1,0:T(8,128)S(1)}, f32[2,256,384]{2,1,0:T(8,128)S(1)}, u32[]{:S(2)}, u32[]{:S(2)}) collective-permute-start(f32[2,256,384]{2,1,0:T(8,128)S(1)} %pad_maximum_fusion), channel_id=1, source_target_pairs={{0,2},{1,3},{2,0},{3,1},{4,6},{5,7},{6,4},{7,5},{8,10},{9,11},{10,... | collective-permute-start | bytes 2359304 | tf_op jit(solution)/shard_map/ppermute | solution.py:289

commit v2 on v1

--- a/solution.py
+++ b/solution.py
@@ -259,6 +259,177 @@
     )(g_lesser, g_greater, onsite, lower, upper, rhs)
 
 
+def halves(x):
+    high = x.astype(jnp.bfloat16)
+    return high, (x - high.astype(jnp.float32)).astype(jnp.bfloat16)
+
+
+def factor(a):
+    return halves(a[0]), halves(a[1]), halves(a[0] + a[1])
+
+
+def three_pass(a, b):
+    dot = lambda u, v: jnp.dot(u, v, preferred_element_type=jnp.float32)
+    return dot(a[0], b[0]) + (dot(a[0], b[1]) + dot(a[1], b[0]))
+
+
+def times(a, b):
+    first, second, third = (three_pass(a[k], b[k]) for k in range(3))
+    return first - second, third - first - second
+
+
+def inverse_of(matrix):
+    eye_rows = lax.broadcasted_iota(jnp.int32, matrix[0].shape, 0)
+    eye_columns = lax.broadcasted_iota(jnp.int32, matrix[0].shape, 1)
+    eye = jnp.where(eye_rows == eye_columns, 1.0, 0.0)
+    scale = 1.0 / diagonal_guess
+    b = eye - matrix[0] * scale, -matrix[1] * scale
+    fb = factor(b)
+    square = times(fb, fb)
+    cube = times(fb, factor(square))
+    return (eye + b[0] + square[0] + cube[0]) * scale, (b[1] + square[1] + cube[1]) * scale
+
+
+def back_kernel(
+    diag, lower, upper, near_lu, near_s, rhs, out, d, s, lu, x, near_x, g, got,
+    direct_send, direct_recv, hop_send, hop_recv, g_send, g_recv,
+):
+    i, count = lax.axis_index("block"), lax.axis_size("block")
+    n, columns = d.shape[-1], s.shape[-1]
+    p, stride = lax.rem(i, 2), count // 2
+    side = 1 - p
+    pair, onward, behind = i + 1 - 2 * p, i + 2 - 4 * p, i - 2 + 4 * p
+    has_onward = jnp.logical_and(onward >= 0, onward < count)
+    has_behind = jnp.logical_and(behind >= 0, behind < count)
+    partner = lax.rem(i + stride, count)
+
+    barrier = pltpu.get_barrier_semaphore()
+    for where in (pair, partner):
+        pl.semaphore_signal(barrier, inc=1, device_id={"block": where}, device_id_type=MESH)
+    for there, where in ((has_onward, onward), (has_behind, behind)):
+
+        @pl.when(there)
+        def _():
+            pl.semaphore_signal(barrier, inc=1, device_id={"block": where}, device_id_type=MESH)
+
+    pl.semaphore_wait(barrier, 2 + has_onward.astype(jnp.int32) + has_behind.astype(jnp.int32))
+
+    def remote(src, dst, send, recv, where):
+        return pltpu.make_async_remote_copy(
+            src_ref=src, dst_ref=dst, send_sem=send, recv_sem=recv, device_id={"block": where}, device_id_type=MESH
+        )
+
+    value = inverse_of((diag[0], diag[1]))
+    x[0], x[1] = value
+    tile = n // 4
+    direct, hops = [], []
+    for k in range(4):
+        rows = pl.ds(k * tile, tile)
+        direct.append(remote(x.at[:, rows], near_x.at[p, :, rows], direct_send.at[k], direct_recv.at[k], pair))
+        hops.append(remote(near_x.at[side, :, rows], near_x.at[p, :, rows], hop_send.at[k], hop_recv.at[k], onward))
+        direct[k].start()
+    d[...] = diag[...]
+    s[...] = rhs[:, 0]
+    for k in (0, 1):
+        lu[0, k], lu[1, k] = lower[k], upper[k]
+    for k in range(4):
+        direct[k].wait_recv()
+
+        @pl.when(has_onward)
+        def _():
+            hops[k].start()
+
+    def update(which, kept):
+        t = factor(times(factor((lu[which, 0], lu[which, 1])), factor((near_x[which, 0], near_x[which, 1]))))
+        v = times(t, factor((near_lu[which, 1 - which, 0], near_lu[which, 1 - which, 1])))
+        r = times(t, factor((near_s[which, 0], near_s[which, 1])))
+        for k in (0, 1):
+            d[k] = d[k] - v[k]
+            s[k] = s[k] - r[k]
+
+        @pl.when(kept)
+        def _():
+            c = times(t, factor((near_lu[which, which, 0], near_lu[which, which, 1])))
+            for k in (0, 1):
+                lu[which, k] = -c[k]
+
+    update(side, has_onward)
+
+    @pl.when(has_behind)
+    def _():
+        for k in range(4):
+            hops[k].wait_recv()
+        update(p, has_behind)
+
+    live = jnp.where(i < stride, 1, 0)
+    inv = factor(inverse_of((d[0], d[1])))
+    chunks = n // columns
+    swaps = [remote(g.at[k], got.at[k], g_send.at[k], g_recv.at[k], partner) for k in range(chunks + 1)]
+    for k in range(chunks + 1):
+        if k == chunks:
+            right = s[0], s[1]
+        else:
+            right = tuple(lu[live, m, :, k * columns : (k + 1) * columns] for m in (0, 1))
+        part = times(inv, factor(right))
+        g[k, 0], g[k, 1] = part
+        swaps[k].start()
+    coupling = factor((lu[live, 0], lu[live, 1]))
+    for k in range(chunks + 1):
+        swaps[k].wait_recv()
+        change = times(coupling, factor((got[k, 0], got[k, 1])))
+        for m in (0, 1):
+            if k == chunks:
+                s[m] = s[m] - change[m]
+            else:
+                cols = slice(k * columns, (k + 1) * columns)
+                d[m, :, cols] = d[m, :, cols] - change[m]
+
+    rows = lax.broadcasted_iota(jnp.int32, (n, n), 0)
+    eye = jnp.where(rows == lax.broadcasted_iota(jnp.int32, (n, n), 1), 1.0, 0.0)
+    scale = 1.0 / diagonal_guess
+    b = factor((eye - d[0] * scale, -d[1] * scale))
+    source = s[0], s[1]
+    value = source
+    for _ in range(3):
+        value = plus(source, times(b, factor(value)))
+    out[0, 0], out[1, 0] = value[0] * scale, value[1] * scale
+    for k in range(4):
+        direct[k].wait_send()
+
+        @pl.when(has_onward)
+        def _():
+            hops[k].wait_send()
+
+    for k in range(chunks + 1):
+        swaps[k].wait_send()
+
+
+def back(diag, lower, upper, near_lu, near_s, rhs):
+    n, columns = diag.shape[-1], rhs.shape[-1]
+    vmem = pl.BlockSpec(memory_space=pltpu.VMEM)
+    f32 = jnp.float32
+    dma = pltpu.SemaphoreType.DMA
+    chunks = n // columns + 1
+    return pl.pallas_call(
+        back_kernel,
+        name="back",
+        out_shape=jax.ShapeDtypeStruct((2, 1, n, columns), f32),
+        in_specs=[vmem] * 6,
+        out_specs=vmem,
+        scratch_shapes=[
+            pltpu.VMEM((2, n, n), f32),
+            pltpu.VMEM((2, n, columns), f32),
+            pltpu.VMEM((2, 2, n, n), f32),
+            pltpu.VMEM((2, n, n), f32),
+            pltpu.VMEM((2, 2, n, n), f32),
+            pltpu.VMEM((chunks, 2, n, columns), f32),
+            pltpu.VMEM((chunks, 2, n, columns), f32),
+            dma((4,)), dma((4,)), dma((4,)), dma((4,)), dma((chunks,)), dma((chunks,)),
+        ],
+        compiler_params=pltpu.CompilerParams(collective_id=1, has_side_effects=True),
+    )(diag, lower, upper, near_lu, near_s, rhs)
+
+
 def shifted(value, steps):
     count = lax.axis_size("block")
     leading, last = max(0, -steps), min(count, count - steps)
@@ -275,6 +446,8 @@
         [jnp.where(index > 0, lower, 0.0), jnp.where(index < count - 1, upper, 0.0)], axis=-1
     )
     diag, near_lu, near_s = front(g_lesser, g_greater, onsite, lower, upper, rhs)
+    if levels == 2:
+        return back(diag, lower, upper, near_lu, near_s, rhs)
     diag = parts(diag)
     first, final = index < 2, index >= count - 2
     low, up = cut(parts(both), 0, n), cut(parts(both), n, 2 * n)

time: 113 us -> 90.9 us (0.80)
  Pallas kernels: 42.5 us -> 89 us
  waiting for transfers between devices: 27.6 us -> 0 us
  matrix products: 20.7 us -> 0 us
  starting transfers between devices: 17.6 us -> 0 us
  other arithmetic: 1.35 us -> 0 us
    pallas_call x0 -> x1, Pallas kernels: none -> 46.5 us  [back(): pl.pallas_call(back_kernel, name='back', out_shape=jax.ShapeDtypeStruct((...]
    ppermute x3 -> x0, waiting for transfers between devices: 27.6 us -> none  [the longest x1 17.8 us: shards(): got = parts(lax.ppermute(jnp.stack(sent), 'block', swap))]
    dot_general x52 -> x0, matrix products: 20.7 us -> none  [real_product(): return jnp.matmul(a, b, precision=MODE)]
    ppermute x3 -> x0, starting transfers between devices: 17.6 us -> none  [the longest x1 11.6 us: shards(): got = parts(lax.ppermute(jnp.stack(sent), 'block', swap))]
  transfers between devices with their start and end apart: 3 -> 0, of which waited for: 2 -> 0; matrix products, arithmetic and copies ran while one was open for 3% -> 0% of each run, Pallas kernels for 0% -> 0%
where the time goes in v2:
time: 90.9 us; the launch traced here: 90.7 us
  Pallas kernels  89 us (98%)
  local copies, waits for them, and re-layouts  1.67 us (2%)
    pallas_call x1, Pallas kernels, back(): pl.pallas_call(back_kernel, name='back', out_shape=jax.ShapeDtypeStruct((...  46.5 us
    pallas_call x1, Pallas kernels, front(): pl.pallas_call(front_kernel, name='front', out_shape=(jax.ShapeDtypeStruc...  42.5 us

profile of v2, /device:TPU:24, one launch (start us, length us, event | category | flops | bytes accessed | tf_op | source)
XLA Modules:
  0.0 90.7 jit_solution(15145144857070183571)
XLA Ops:
  0.0 42.5 %front.1 = (f32[2,256,256]{2,1,0:T(8,128)}, f32[2,2,2,256,256]{4,3,2,1,0:T(8,128)}, f32[2,2,256,128]{3,2,1,0:T(8,128)}) custom-call(f32[2,1,256,256]{3,2,1,0:T(8,128)} %gl.1, f32[2,1,256,256]{3,2,1,0:T(8,128)} %gg.1, f32[2,1,256,256]{3,2,1,0:T(8,128)} %onsite.1, f32[2,256,256]{2,1,0:T(8,128)} %lower.3, f32[2,256,256]{2,1,0:T(8,128)} %upper.3, ...), custom_call_target="tpu_custom_call" | custom-call | tf_op jit(solution)/shard_map/front/pallas_call | solution.py:241
  42.5 46.5 %back.1 = f32[2,1,256,128]{3,2,1,0:T(8,128)} custom-call(f32[2,256,256]{2,1,0:T(8,128)} %get-tuple-element.8.diag, f32[2,256,256]{2,1,0:T(8,128)} %lower.3, f32[2,256,256]{2,1,0:T(8,128)} %upper.3, f32[2,2,2,256,256]{4,3,2,1,0:T(8,128)} %get-tuple-element.9.near_lu, f32[2,2,256,128]{3,2,1,0:T(8,128)} %get-tuple-element.10.near_s, f32[2,1,256,128]{3,2,1,0:T(8,128)} %rhs.3), custom_call_target="tpu_custom_call" | custom-call | tf_op jit(solution)/shard_map/back/pallas_call | solution.py:413
  89.0 1.7 %copy.8 = f32[2,1,256,128]{3,2,1,0:T(8,128)} copy(f32[2,1,256,128]{3,2,1,0:T(8,128)} %back.1) | data formatting | bytes 524288

commit v3 on v2

--- a/solution.py
+++ b/solution.py
@@ -72,7 +72,7 @@
     gl, gg, onsite, lower, upper, rhs, diag, near_lu, near_s,
     lu, gl_all, gg_all, res, pol,
     in_send, in_recv, out_send, out_recv, lu_send, lu_recv, hop_send, hop_recv,
-    mate_send, mate_recv, local,
+    mate_send, mate_recv, local, rows_out=None, partner=None,
 ):
     e, i = lax.axis_index("energy"), lax.axis_index("block")
     energies, count = lax.axis_size("energy"), lax.axis_size("block")
@@ -99,7 +99,11 @@
     def _():
         pl.semaphore_signal(barrier, inc=1, device_id={"block": behind}, device_id_type=MESH)
 
-    pl.semaphore_wait(barrier, energies + has_onward.astype(jnp.int32) + has_behind.astype(jnp.int32))
+    peers = energies
+    if partner is not None:
+        peers = energies + 1
+        pl.semaphore_signal(barrier, inc=1, device_id={"block": partner}, device_id_type=MESH)
+    pl.semaphore_wait(barrier, peers + has_onward.astype(jnp.int32) + has_behind.astype(jnp.int32))
 
     def remote(src, dst, send, recv, **where):
         return pltpu.make_async_remote_copy(
@@ -193,6 +197,13 @@
             if k < 2:
                 shared[2 + k].start()
 
+    def hand_on(q):
+        rows_out[0][q].wait_recv()
+
+        @pl.when(has_onward)
+        def _():
+            rows_out[1][q].start()
+
     keep.wait()
     for q in range(energies):
 
@@ -203,6 +214,12 @@
         rows = pl.ds(q * share, share)
         for k in (0, 1):
             diag[k, rows] = onsite[k, 0, rows] - pol[q, k]
+        if rows_out is not None:
+            rows_out[0][q].start()
+            if q > 0:
+                hand_on(q - 1)
+    if rows_out is not None:
+        hand_on(energies - 1)
 
     for k in range(2):
         shared[k].wait_recv()
@@ -290,11 +307,15 @@
     return (eye + b[0] + square[0] + cube[0]) * scale, (b[1] + square[1] + cube[1]) * scale
 
 
-def back_kernel(
-    diag, lower, upper, near_lu, near_s, rhs, out, d, s, lu, x, near_x, g, got,
-    direct_send, direct_recv, hop_send, hop_recv, g_send, g_recv,
+def whole_kernel(
+    gl, gg, onsite, lower, upper, rhs, out, diag, near_lu, near_s,
+    lu, gl_all, gg_all, res, pol,
+    in_send, in_recv, out_send, out_recv, lu_send, lu_recv, piece_send, piece_recv,
+    mate_send, mate_recv, local,
+    d, s, near_d, g, got, direct_send, direct_recv, hop_send, hop_recv, g_send, g_recv,
 ):
     i, count = lax.axis_index("block"), lax.axis_size("block")
+    energies = lax.axis_size("energy")
     n, columns = d.shape[-1], s.shape[-1]
     p, stride = lax.rem(i, 2), count // 2
     side = 1 - p
@@ -303,44 +324,30 @@
     has_behind = jnp.logical_and(behind >= 0, behind < count)
     partner = lax.rem(i + stride, count)
 
-    barrier = pltpu.get_barrier_semaphore()
-    for where in (pair, partner):
-        pl.semaphore_signal(barrier, inc=1, device_id={"block": where}, device_id_type=MESH)
-    for there, where in ((has_onward, onward), (has_behind, behind)):
-
-        @pl.when(there)
-        def _():
-            pl.semaphore_signal(barrier, inc=1, device_id={"block": where}, device_id_type=MESH)
-
-    pl.semaphore_wait(barrier, 2 + has_onward.astype(jnp.int32) + has_behind.astype(jnp.int32))
-
     def remote(src, dst, send, recv, where):
         return pltpu.make_async_remote_copy(
             src_ref=src, dst_ref=dst, send_sem=send, recv_sem=recv, device_id={"block": where}, device_id_type=MESH
         )
 
-    value = inverse_of((diag[0], diag[1]))
-    x[0], x[1] = value
-    tile = n // 4
+    tile = n // energies
     direct, hops = [], []
-    for k in range(4):
+    for k in range(energies):
         rows = pl.ds(k * tile, tile)
-        direct.append(remote(x.at[:, rows], near_x.at[p, :, rows], direct_send.at[k], direct_recv.at[k], pair))
-        hops.append(remote(near_x.at[side, :, rows], near_x.at[p, :, rows], hop_send.at[k], hop_recv.at[k], onward))
-        direct[k].start()
+        direct.append(remote(diag.at[:, rows], near_d.at[p, :, rows], direct_send.at[k], direct_recv.at[k], pair))
+        hops.append(
+            remote(near_d.at[side, :, rows], near_d.at[p, :, rows], hop_send.at[k], hop_recv.at[k], onward)
+        )
+    front_kernel(
+        gl, gg, onsite, lower, upper, rhs, diag, near_lu, near_s,
+        lu, gl_all, gg_all, res, pol,
+        in_send, in_recv, out_send, out_recv, lu_send, lu_recv, piece_send, piece_recv,
+        mate_send, mate_recv, local, (direct, hops), partner,
+    )
     d[...] = diag[...]
     s[...] = rhs[:, 0]
-    for k in (0, 1):
-        lu[0, k], lu[1, k] = lower[k], upper[k]
-    for k in range(4):
-        direct[k].wait_recv()
-
-        @pl.when(has_onward)
-        def _():
-            hops[k].start()
 
     def update(which, kept):
-        t = factor(times(factor((lu[which, 0], lu[which, 1])), factor((near_x[which, 0], near_x[which, 1]))))
+        t = factor(times(factor((lu[which, 0], lu[which, 1])), factor(inverse_of((near_d[which, 0], near_d[which, 1])))))
         v = times(t, factor((near_lu[which, 1 - which, 0], near_lu[which, 1 - which, 1])))
         r = times(t, factor((near_s[which, 0], near_s[which, 1])))
         for k in (0, 1):
@@ -357,7 +364,7 @@
 
     @pl.when(has_behind)
     def _():
-        for k in range(4):
+        for k in range(energies):
             hops[k].wait_recv()
         update(p, has_behind)
 
@@ -393,7 +400,7 @@
     for _ in range(3):
         value = plus(source, times(b, factor(value)))
     out[0, 0], out[1, 0] = value[0] * scale, value[1] * scale
-    for k in range(4):
+    for k in range(energies):
         direct[k].wait_send()
 
         @pl.when(has_onward)
@@ -404,30 +411,39 @@
         swaps[k].wait_send()
 
 
-def back(diag, lower, upper, near_lu, near_s, rhs):
-    n, columns = diag.shape[-1], rhs.shape[-1]
+def whole(g_lesser, g_greater, onsite, lower, upper, rhs):
+    energies = lax.axis_size("energy")
+    n, columns = onsite.shape[2], rhs.shape[-1]
     vmem = pl.BlockSpec(memory_space=pltpu.VMEM)
     f32 = jnp.float32
     dma = pltpu.SemaphoreType.DMA
     chunks = n // columns + 1
+    pieces = pltpu.VMEM((energies, 2, n // energies, n), f32)
     return pl.pallas_call(
-        back_kernel,
-        name="back",
+        whole_kernel,
+        name="whole",
         out_shape=jax.ShapeDtypeStruct((2, 1, n, columns), f32),
         in_specs=[vmem] * 6,
         out_specs=vmem,
         scratch_shapes=[
             pltpu.VMEM((2, n, n), f32),
+            pltpu.VMEM((2, 2, 2, n, n), f32),
+            pltpu.VMEM((2, 2, n, columns), f32),
+            pltpu.VMEM((2, 2, n, n), f32),
+            pieces, pieces, pieces, pieces,
+            dma((2, energies)), dma((2, energies)), dma((energies,)), dma((energies,)),
+            dma((3,)), dma((3,)), dma((3,)), dma((3,)),
+            dma((2, 2)), dma((2, 2)), dma((2,)),
+            pltpu.VMEM((2, n, n), f32),
             pltpu.VMEM((2, n, columns), f32),
-            pltpu.VMEM((2, 2, n, n), f32),
-            pltpu.VMEM((2, n, n), f32),
             pltpu.VMEM((2, 2, n, n), f32),
             pltpu.VMEM((chunks, 2, n, columns), f32),
             pltpu.VMEM((chunks, 2, n, columns), f32),
-            dma((4,)), dma((4,)), dma((4,)), dma((4,)), dma((chunks,)), dma((chunks,)),
+            dma((energies,)), dma((energies,)), dma((energies,)), dma((energies,)),
+            dma((chunks,)), dma((chunks,)),
         ],
         compiler_params=pltpu.CompilerParams(collective_id=1, has_side_effects=True),
-    )(diag, lower, upper, near_lu, near_s, rhs)
+    )(g_lesser, g_greater, onsite, lower, upper, rhs)
 
 
 def shifted(value, steps):
@@ -445,9 +461,9 @@
     both = jnp.concatenate(
         [jnp.where(index > 0, lower, 0.0), jnp.where(index < count - 1, upper, 0.0)], axis=-1
     )
+    if levels == 2:
+        return whole(g_lesser, g_greater, onsite, lower, upper, rhs)
     diag, near_lu, near_s = front(g_lesser, g_greater, onsite, lower, upper, rhs)
-    if levels == 2:
-        return back(diag, lower, upper, near_lu, near_s, rhs)
     diag = parts(diag)
     first, final = index < 2, index >= count - 2
     low, up = cut(parts(both), 0, n), cut(parts(both), n, 2 * n)

time: 90.9 us -> 82.8 us (0.911)
  Pallas kernels: 89 us -> 81 us
    pallas_call x2 -> x1, Pallas kernels: 89 us -> 81 us  [whole(): pl.pallas_call(whole_kernel, name='whole', out_shape=jax.ShapeDtypeStruct...]
where the time goes in v3:
time: 82.8 us; the launch traced here: 82.7 us
  Pallas kernels  81 us (98%)
  local copies, waits for them, and re-layouts  1.67 us (2%)
    pallas_call x1, Pallas kernels, whole(): pl.pallas_call(whole_kernel, name='whole', out_shape=jax.ShapeDtypeStruct...  81 us
    unnamed x1, local copies, waits for them, and re-layouts  1.67 us

profile of v3, /device:TPU:24, one launch (start us, length us, event | category | flops | bytes accessed | tf_op | source)
XLA Modules:
  0.0 82.7 jit_solution(3848075066337333760)
XLA Ops:
  0.0 81.0 %whole.1 = f32[2,1,256,128]{3,2,1,0:T(8,128)} custom-call(f32[2,1,256,256]{3,2,1,0:T(8,128)} %gl.1, f32[2,1,256,256]{3,2,1,0:T(8,128)} %gg.1, f32[2,1,256,256]{3,2,1,0:T(8,128)} %onsite.1, f32[2,256,256]{2,1,0:T(8,128)} %lower.1, f32[2,256,256]{2,1,0:T(8,128)} %upper.1, f32[2,1,256,128]{3,2,1,0:T(8,128)} %rhs.1), custom_call_target="tpu_custom_call" | custom-call | tf_op jit(solution)/shard_map/whole/pallas_call | solution.py:422
  81.0 1.7 %copy.8 = f32[2,1,256,128]{3,2,1,0:T(8,128)} copy(f32[2,1,256,128]{3,2,1,0:T(8,128)} %whole.1) | data formatting | bytes 524288

commit v4 on v3

--- a/solution.py
+++ b/solution.py
@@ -110,22 +110,29 @@
             src_ref=src, dst_ref=dst, send_sem=send, recv_sem=recv, device_id=where, device_id_type=MESH
         )
 
-    def in_copy(k, q, source):
+    part = share // 2
+
+    def in_copy(h, k, q, source):
         src, dst = ((gl, gl_all), (gg, gg_all))[k]
-        rows = src.at[:, 0, pl.ds(q * share, share), :]
-        return remote(rows, dst.at[source], in_send.at[k, q], in_recv.at[k, source], energy=q)
-
-    def out_copy(w, source):
-        return remote(res.at[w], pol.at[source], out_send.at[w], out_recv.at[source], energy=w)
+        rows = src.at[:, 0, pl.ds(q * share + h * part, part), :]
+        there = dst.at[source, :, pl.ds(h * part, part), :]
+        return remote(rows, there, in_send.at[h, k, q], in_recv.at[h, k, source], energy=q)
+
+    def out_copy(h, w, source):
+        rows = pl.ds(h * part, part)
+        return remote(
+            res.at[w, :, rows, :], pol.at[source, :, rows, :], out_send.at[h, w], out_recv.at[h, source], energy=w
+        )
 
     for copy in fill:
         copy.wait()
-    for k in (0, 1):
-        for q in range(energies):
-
-            @pl.when(q != e)
-            def _():
-                in_copy(k, q, e).start()
+    for h in (0, 1):
+        for k in (0, 1):
+            for q in range(energies):
+
+                @pl.when(q != e)
+                def _():
+                    in_copy(h, k, q, e).start()
 
     own = []
     for k, (src, dst) in enumerate(((gl, gl_all), (gg, gg_all))):
@@ -159,33 +166,34 @@
 
     for copy in own:
         copy.wait()
-    for k in (0, 1):
-        for q in range(energies):
-
-            @pl.when(q != e)
+    scale = 1.0 / math.sqrt(energies)
+    for h in (0, 1):
+        for k in (0, 1):
+            for q in range(energies):
+
+                @pl.when(q != e)
+                def _():
+                    in_copy(h, k, q, q).wait_recv()
+
+        for w in range(energies):
+
+            def step(row, carry, w=w, h=h):
+                rows = pl.ds(pl.multiple_of(h * part + row * 8, 8), 8)
+                real = imag = None
+                for k in range(w, energies):
+                    a, b = gl_all[k, 0, rows], gl_all[k, 1, rows]
+                    x, y = gg_all[k - w, 0, rows], gg_all[k - w, 1, rows]
+                    s, t = a * x - b * y, a * y + b * x
+                    real, imag = (s, t) if real is None else (real + s, imag + t)
+                res[w, 0, rows] = real * scale
+                res[w, 1, rows] = imag * scale
+                return carry
+
+            lax.fori_loop(0, part // 8, step, 0)
+
+            @pl.when(w != e)
             def _():
-                in_copy(k, q, q).wait_recv()
-
-    scale = 1.0 / math.sqrt(energies)
-    for w in list(range(energies)):
-
-        def step(row, carry, w=w):
-            rows = pl.ds(pl.multiple_of(row * 8, 8), 8)
-            real = imag = None
-            for k in range(w, energies):
-                a, b = gl_all[k, 0, rows], gl_all[k, 1, rows]
-                x, y = gg_all[k - w, 0, rows], gg_all[k - w, 1, rows]
-                s, t = a * x - b * y, a * y + b * x
-                real, imag = (s, t) if real is None else (real + s, imag + t)
-            res[w, 0, rows] = real * scale
-            res[w, 1, rows] = imag * scale
-            return carry
-
-        lax.fori_loop(0, share // 8, step, 0)
-
-        @pl.when(w != e)
-        def _():
-            out_copy(w, e).start()
+                out_copy(h, w, e).start()
 
     keep = pltpu.make_async_copy(res.at[e], pol.at[e], local.at[0])
     keep.start()
@@ -209,7 +217,8 @@
 
         @pl.when(q != e)
         def _():
-            out_copy(q, q).wait_recv()
+            out_copy(0, q, q).wait_recv()
+            out_copy(1, q, q).wait_recv()
 
         rows = pl.ds(q * share, share)
         for k in (0, 1):
@@ -242,9 +251,10 @@
 
         @pl.when(q != e)
         def _():
-            in_copy(0, q, e).wait_send()
-            in_copy(1, q, e).wait_send()
-            out_copy(q, e).wait_send()
+            for h in (0, 1):
+                in_copy(h, 0, q, e).wait_send()
+                in_copy(h, 1, q, e).wait_send()
+                out_copy(h, q, e).wait_send()
 
 
 def front(g_lesser, g_greater, onsite, lower, upper, rhs):
@@ -268,7 +278,7 @@
         scratch_shapes=[
             pltpu.VMEM((2, 2, n, n), f32),
             pieces, pieces, pieces, pieces,
-            dma((2, energies)), dma((2, energies)), dma((energies,)), dma((energies,)),
+            dma((2, 2, energies)), dma((2, 2, energies)), dma((2, energies)), dma((2, energies)),
             dma((3,)), dma((3,)), dma((3,)), dma((3,)),
             dma((2, 2)), dma((2, 2)), dma((2,)),
         ],
@@ -431,7 +441,7 @@
             pltpu.VMEM((2, 2, n, columns), f32),
             pltpu.VMEM((2, 2, n, n), f32),
             pieces, pieces, pieces, pieces,
-            dma((2, energies)), dma((2, energies)), dma((energies,)), dma((energies,)),
+            dma((2, 2, energies)), dma((2, 2, energies)), dma((2, energies)), dma((2, energies)),
             dma((3,)), dma((3,)), dma((3,)), dma((3,)),
             dma((2, 2)), dma((2, 2)), dma((2,)),
             pltpu.VMEM((2, n, n), f32),

time: 82.8 us -> 82 us (level)
    pallas_call x1, Pallas kernels: 81 us -> 80.2 us  [whole(): pl.pallas_call(whole_kernel, name='whole', out_shape=jax.ShapeDtypeStruct...]
where the time goes in v4:
time: 82 us; the launch traced here: 81.8 us
  Pallas kernels  80.2 us (98%)
  local copies, waits for them, and re-layouts  1.67 us (2%)
    pallas_call x1, Pallas kernels, whole(): pl.pallas_call(whole_kernel, name='whole', out_shape=jax.ShapeDtypeStruct...  80.2 us
    unnamed x1, local copies, waits for them, and re-layouts  1.67 us

profile of v4, /device:TPU:24, one launch (start us, length us, event | category | flops | bytes accessed | tf_op | source)
XLA Modules:
  0.0 81.8 jit_solution(11442038908886487848)
XLA Ops:
  0.0 80.2 %whole.1 = f32[2,1,256,128]{3,2,1,0:T(8,128)} custom-call(f32[2,1,256,256]{3,2,1,0:T(8,128)} %gl.1, f32[2,1,256,256]{3,2,1,0:T(8,128)} %gg.1, f32[2,1,256,256]{3,2,1,0:T(8,128)} %onsite.1, f32[2,256,256]{2,1,0:T(8,128)} %lower.1, f32[2,256,256]{2,1,0:T(8,128)} %upper.1, f32[2,1,256,128]{3,2,1,0:T(8,128)} %rhs.1), custom_call_target="tpu_custom_call" | custom-call | tf_op jit(solution)/shard_map/whole/pallas_call | solution.py:432
  80.2 1.7 %copy.8 = f32[2,1,256,128]{3,2,1,0:T(8,128)} copy(f32[2,1,256,128]{3,2,1,0:T(8,128)} %whole.1) | data formatting | bytes 524288

commit v5 on v4

--- a/solution.py
+++ b/solution.py
@@ -391,25 +391,17 @@
         g[k, 0], g[k, 1] = part
         swaps[k].start()
     coupling = factor((lu[live, 0], lu[live, 1]))
-    for k in range(chunks + 1):
+    for k in range(chunks):
         swaps[k].wait_recv()
         change = times(coupling, factor((got[k, 0], got[k, 1])))
+        cols = slice(k * columns, (k + 1) * columns)
         for m in (0, 1):
-            if k == chunks:
-                s[m] = s[m] - change[m]
-            else:
-                cols = slice(k * columns, (k + 1) * columns)
-                d[m, :, cols] = d[m, :, cols] - change[m]
-
-    rows = lax.broadcasted_iota(jnp.int32, (n, n), 0)
-    eye = jnp.where(rows == lax.broadcasted_iota(jnp.int32, (n, n), 1), 1.0, 0.0)
-    scale = 1.0 / diagonal_guess
-    b = factor((eye - d[0] * scale, -d[1] * scale))
-    source = s[0], s[1]
-    value = source
-    for _ in range(3):
-        value = plus(source, times(b, factor(value)))
-    out[0, 0], out[1, 0] = value[0] * scale, value[1] * scale
+            d[m, :, cols] = d[m, :, cols] - change[m]
+    final = factor(inverse_of((d[0], d[1])))
+    swaps[chunks].wait_recv()
+    change = times(coupling, factor((got[chunks, 0], got[chunks, 1])))
+    value = times(final, factor((s[0] - change[0], s[1] - change[1])))
+    out[0, 0], out[1, 0] = value
     for k in range(energies):
         direct[k].wait_send()
 

time: 82 us -> 81.3 us (level)
  no operation moved by 1% of the time
where the time goes in v5:
time: 81.3 us; the launch traced here: 81.1 us
  Pallas kernels  79.4 us (98%)
  local copies, waits for them, and re-layouts  1.67 us (2%)
    pallas_call x1, Pallas kernels, whole(): pl.pallas_call(whole_kernel, name='whole', out_shape=jax.ShapeDtypeStruct...  79.4 us
    unnamed x1, local copies, waits for them, and re-layouts  1.67 us

profile of v5, /device:TPU:24, one launch (start us, length us, event | category | flops | bytes accessed | tf_op | source)
XLA Modules:
  0.0 81.1 jit_solution(2508420260571269593)
XLA Ops:
  0.0 79.4 %whole.1 = f32[2,1,256,128]{3,2,1,0:T(8,128)} custom-call(f32[2,1,256,256]{3,2,1,0:T(8,128)} %gl.1, f32[2,1,256,256]{3,2,1,0:T(8,128)} %gg.1, f32[2,1,256,256]{3,2,1,0:T(8,128)} %onsite.1, f32[2,256,256]{2,1,0:T(8,128)} %lower.1, f32[2,256,256]{2,1,0:T(8,128)} %upper.1, f32[2,1,256,128]{3,2,1,0:T(8,128)} %rhs.1), custom_call_target="tpu_custom_call" | custom-call | tf_op jit(solution)/shard_map/whole/pallas_call | solution.py:424
  79.4 1.7 %copy.8 = f32[2,1,256,128]{3,2,1,0:T(8,128)} copy(f32[2,1,256,128]{3,2,1,0:T(8,128)} %whole.1) | data formatting | bytes 524288
